TPU v7x, 32 devices: a whole 2x2x4 slice. The times are simulated.
32 devices in a mesh: gx: 4 (over y, x), gy: 2 (over core), gz: 4 (over z).
Axes of the slice: x: 2, y: 2, z: 4, core: 2. Of those that a mesh axis runs over, the one named last changes fastest.
Arguments:
- tokens: bfloat16 [192, 12288], P(('gy', 'gz'), 'gx'), may hold values from -6 to 6
- grad_out: bfloat16 [192, 12288], P(('gy', 'gz'), 'gx'), may hold values from -0.86328125 to 0.86328125
- w_in: bfloat16 [12288, 24576], P('gx', ('gy', 'gz')), may hold values from -0.0546875 to 0.0546875
- w_out: bfloat16 [24576, 12288], P(('gy', 'gz'), 'gx'), may hold values from -0.0390625 to 0.0390625
Outputs:
- output: float32 [192, 12288], P(('gy', 'gz'), 'gx')
- grad_in: float32 [192, 12288], P(('gy', 'gz'), 'gx')
- grad_w_in: bfloat16 [12288, 24576], P('gx', ('gy', 'gz'))
- grad_w_out: bfloat16 [24576, 12288], P(('gy', 'gz'), 'gx')
All inputs are finite; a program needn't handle non-finite values.
Results may differ from a plain program's by a relative error of at most 0.0049.
Values may be sent and summed in bfloat16 or wider, within the bound.
A program may use at most 128 MiB of HBM per device.

v0:
```python
import jax
import jax.numpy as jnp
from jax import lax
from jax.sharding import PartitionSpec as P


def activate(pre_sum, back_sum):
    scale_c = 0.7978845608
    inner_arg = scale_c * (pre_sum + 0.044715 * pre_sum * pre_sum * pre_sum)
    tanh_val = jnp.tanh(inner_arg)
    value = 0.5 * pre_sum * (1.0 + tanh_val)
    deriv = 0.5 * (1.0 + tanh_val) + 0.5 * pre_sum * (1.0 - tanh_val * tanh_val) * scale_c * (
        1.0 + 3.0 * 0.044715 * pre_sum * pre_sum
    )
    return (value.astype(jnp.bfloat16), (back_sum * deriv).astype(jnp.bfloat16))


def right_product(left, right):
    return lax.dot_general(
        left, right, (((1,), (1,)), ((), ())), preferred_element_type=jnp.float32
    )


def left_product(left, right):
    return lax.dot_general(
        left, right, (((0,), (0,)), ((), ())), preferred_element_type=jnp.float32
    )


def shards(tokens, grad_out, w_in, w_out):
    token_rows, grad_rows = (
        lax.all_gather(tokens, ("gy", "gz"), axis=0, tiled=True),
        lax.all_gather(grad_out, ("gy", "gz"), axis=0, tiled=True),
    )
    pre_part = jnp.dot(token_rows, w_in, preferred_element_type=jnp.float32)
    back_part = right_product(grad_rows, w_out)
    pre_sum, back_sum = lax.psum((pre_part, back_part), "gx")
    hidden, slopes = activate(pre_sum, back_sum)
    picked = hidden
    output = lax.psum_scatter(
        jnp.dot(picked, w_out, preferred_element_type=jnp.float32),
        ("gy", "gz"),
        scatter_dimension=0,
        tiled=True,
    )
    picked = slopes
    grad_in = lax.psum_scatter(
        right_product(picked, w_in), ("gy", "gz"), scatter_dimension=0, tiled=True
    )
    grad_w_in = left_product(token_rows, slopes).astype(jnp.bfloat16)
    grad_w_out = left_product(hidden, grad_rows).astype(jnp.bfloat16)
    return (output, grad_in, grad_w_in, grad_w_out)


def solution(mesh):
    placed = (
        P(("gy", "gz"), "gx"),
        P(("gy", "gz"), "gx"),
        P("gx", ("gy", "gz")),
        P(("gy", "gz"), "gx"),
    )
    return jax.shard_map(
        shards,
        mesh=mesh,
        in_specs=placed,
        out_specs=(
            P(("gy", "gz"), "gx"),
            P(("gy", "gz"), "gx"),
            P("gx", ("gy", "gz")),
            P(("gy", "gz"), "gx"),
        ),
        check_vma=False,
    )
```

profile of v0, /device:TPU:0, one launch (start us, length us, event | category | flops | bytes accessed | tf_op | source)
XLA Modules:
  0.0 315.6 jit_solution(16967540374349955192)
XLA Ops:
  7.2 0.0 all-gather.3.cloned.1.call-start
  7.2 0.7 all-gather.3.cloned.1.call-update
  7.9 0.0 all-gather.5.cloned.1.call-start
  7.9 0.7 all-gather.5.cloned.1.call-update
  8.6 0.0 all-reduce.3.cloned.1.call-start
  8.7 26.3 %all-gather.3.cloned.1.call-done = bf16[192,3072]{1,0:T(8,128)(2,1)} async-done(((bf16[24,3072]{1,0:T(8,128)(2,1)}), bf16[192,3072]{1,0:T(8,128)(2,1)}) %all-gather.3.cloned.1.call-update) | async-done | bytes 1179664 | tf_op jit(solution)/shard_map/all_gather | solution.py:32
  35.0 12.0 %fusion.8 = f32[192,3072]{1,0:T(8,128)} fusion(bf16[192,3072]{1,0:T(8,128)(2,1)} %all-gather.3.cloned.1.call-done, bf16[3072,3072]{1,0:T(8,128)(2,1)} %param.6), kind=kOutput, calls=%fused_computation.13 | convolution fusion | flops 3623878656 | bytes 22413312 | tf_op jit(solution)/shard_map/dot_general | solution.py:35
  47.0 12.1 %all-gather.5.cloned.1.call-done = bf16[192,3072]{1,0:T(8,128)(2,1)} async-done(((bf16[24,3072]{1,0:T(8,128)(2,1)}), bf16[192,3072]{1,0:T(8,128)(2,1)}) %all-gather.5.cloned.1.call-update) | async-done | bytes 1179664 | tf_op jit(solution)/shard_map/all_gather | solution.py:33
  59.0 14.5 %fusion.9 = f32[192,3072]{1,0:T(8,128)} fusion(bf16[192,3072]{1,0:T(8,128)(2,1)} %all-gather.5.cloned.1.call-done, bf16[3072,3072]{1,0:T(8,128)(2,1)} %param.7), kind=kOutput, calls=%fused_computation.14 | convolution fusion | flops 3623878656 | bytes 22413312 | tf_op jit(solution)/shard_map/dot_general | solution.py:19
  73.5 0.0 all-reduce.3.cloned.1.call-update
  73.6 0.0 reduce-scatter.3.cloned.1.call-start
  73.6 112.7 %all-reduce.3.cloned.1.call-done = (f32[192,3072]{1,0:T(8,128)}, f32[192,3072]{1,0:T(8,128)}) async-done(((f32[192,3072]{1,0:T(8,128)}, f32[192,3072]{1,0:T(8,128)}), (f32[192,3072]{1,0:T(8,128)}, f32[192,3072]{1,0:T(8,128)})) %all-reduce.3.cloned.1.call-update) | async-done | bytes 4718608 | tf_op jit(solution)/shard_map/psum | solution.py:37
  186.3 12.6 %fusion.7 = f32[192,3072]{1,0:T(8,128)} fusion(bf16[3072,3072]{1,0:T(8,128)(2,1)} %param.7, f32[192,3072]{1,0:T(8,128)} %get-tuple-element.8), kind=kOutput, calls=%fused_computation.12 | convolution fusion | flops 3629187072 | bytes 23592960 | tf_op jit(solution)/shard_map/dot_general | solution.py:41
  198.9 0.0 copy-start
  198.9 0.0 reduce-scatter.3.cloned.1.call-update
  198.9 0.2 reduce-scatter.5.cloned.1.call-start
  199.2 1.4 copy-done
  200.6 3.1 fusion.6
  203.7 11.7 %fusion.10 = f32[192,3072]{1,0:T(8,128)} fusion(bf16[192,3072]{1,0:T(8,128)(2,1)S(1)} %fusion.6, bf16[3072,3072]{1,0:T(8,128)(2,1)} %param.6), kind=kOutput, calls=%fused_computation.15 | convolution fusion | flops 3623878656 | bytes 22413312 | tf_op jit(solution)/shard_map/dot_general | solution.py:19
  215.5 0.0 reduce-scatter.5.cloned.1.call-update
  215.5 10.8 %convert_bitcast_fusion = bf16[3072,3072]{0,1:T(8,128)(2,1)} fusion(bf16[192,3072]{1,0:T(8,128)(2,1)S(1)} %fusion.6, bf16[192,3072]{1,0:T(8,128)(2,1)} %all-gather.3.cloned.1.call-done), kind=kOutput, calls=%fused_computation | convolution fusion | flops 3633315840 | bytes 21233664 | tf_op jit(solution)/shard_map/dot_general | solution.py:25
  226.3 0.0 copy-start.1
  226.3 24.7 %copy.8 = bf16[3072,3072]{1,0:T(8,128)(2,1)} copy(bf16[3072,3072]{0,1:T(8,128)(2,1)} %convert_bitcast_fusion) | data formatting | bytes 37748736
  251.0 0.0 copy-done.1
  251.0 9.6 %convolution_convert_fusion = bf16[3072,3072]{1,0:T(8,128)(2,1)} fusion(bf16[192,3072]{1,0:T(8,128)(2,1)S(1)} %copy-done.1, f32[192,3072]{1,0:T(8,128)S(1)} %copy-done), kind=kOutput, calls=%fused_computation.1 | convolution fusion | flops 3638624256 | bytes 22413312 | tf_op jit(solution)/shard_map/dot_general | solution.py:25
  260.6 0.0 reduce-scatter.3.cloned.1.call-done
  260.6 48.5 %reduce-scatter.5.cloned.1.call-done = f32[24,3072]{1,0:T(8,128)} async-done(((f32[192,3072]{1,0:T(8,128)}), f32[24,3072]{1,0:T(8,128)}) %reduce-scatter.5.cloned.1.call-update) | async-done | bytes 294928 | tf_op jit(solution)/shard_map/reduce_scatter | solution.py:47
Async XLA Ops:
  7.2 27.8 %all-gather.3.cloned.1.call-start = ((), (), s32[]{:S(2)}) async-start(), calls=%async_computation.2 | async-start | bytes 1327104 | tf_op jit(solution)/shard_map/all_gather | solution.py:32
  7.9 51.1 %all-gather.5.cloned.1.call-start = ((), (), s32[]{:S(2)}) async-start(), calls=%async_computation.4 | async-start | bytes 1327104 | tf_op jit(solution)/shard_map/all_gather | solution.py:33
  8.6 177.7 %all-reduce.3.cloned.1.call-start = ((), (), s32[]{:S(2)}) async-start(), calls=%async_computation.6 | async-start | bytes 9437184 | tf_op jit(solution)/shard_map/psum | solution.py:37
  73.6 187.0 %reduce-scatter.3.cloned.1.call-start = ((), (), s32[]{:S(2)}) async-start(), calls=%async_computation.3 | async-start | bytes 2654208 | tf_op jit(solution)/shard_map/reduce_scatter | solution.py:40
  198.9 1.7 copy-start
  198.9 110.1 %reduce-scatter.5.cloned.1.call-start = ((), (), s32[]{:S(2)}) async-start(), calls=%async_computation.5 | async-start | bytes 2654208 | tf_op jit(solution)/shard_map/reduce_scatter | solution.py:47
  226.3 24.7 %copy-start.1 = (bf16[192,3072]{1,0:T(8,128)(2,1)S(1)}, bf16[192,3072]{1,0:T(8,128)(2,1)}, u32[]{:S(2)}) copy-start(bf16[192,3072]{1,0:T(8,128)(2,1)} %all-gather.5.cloned.1.call-done) | copy-start | bytes 3538948
Sparse Core Ops, SparseCore 0:
  9.6 25.3 all-gather.2
  36.6 22.4 all-gather.4
  73.7 112.6 all-reduce.2
  199.1 54.0 reduce-scatter.2
  255.9 53.1 reduce-scatter.4
where the time goes:
time: 316 us
  waiting for transfers between devices  201 us (64%)
  matrix products  71.1 us (22%)
  local copies, waits for them, and re-layouts  26.1 us (8%)
  between operations  13.8 us (4%)
    psum x1, waiting for transfers between devices, shards(): pre_sum, back_sum = lax.psum((pre_part, back_part), 'gx')  113 us
    reduce_scatter x1, waiting for transfers between devices, shards(): lax.psum_scatter(right_product(picked, w_in), ('gy', 'gz'), scatter_dimen...  48.5 us
    all_gather x1, waiting for transfers between devices, shards(): lax.all_gather(tokens, ('gy', 'gz'), axis=0, tiled=True)  26.3 us
    dot_general x2, matrix products, right_product(): lax.dot_general(left, right, (((1,), (1,)), ((), ())), preferred_element_...  26.2 us
    unnamed x5, local copies, waits for them, and re-layouts  26.1 us
    dot_general x2, matrix products, left_product(): lax.dot_general(left, right, (((0,), (0,)), ((), ())), preferred_element_...  20.4 us
    dot_general x1, matrix products, shards(): jnp.dot(picked, w_out, preferred_element_type=jnp.float32)  12.6 us
    all_gather x1, waiting for transfers between devices, shards(): lax.all_gather(grad_out, ('gy', 'gz'), axis=0, tiled=True)  12.1 us
  transfers between devices with their start and end apart: 5, of which 4 were waited for; matrix products, arithmetic and copies ran while one was open for 23% of the time, Pallas kernels for 0%

commit v1 on v0

v1 whole, which is shorter than its diff:
```python
import functools
import math

import jax
import jax.numpy as jnp
from jax import lax
from jax.experimental import pallas as pl
from jax.experimental.pallas import tpu as pltpu
from jax.sharding import PartitionSpec as P

MESH = pl.DeviceIdType.MESH
NN = (((1,), (0,)), ((), ()))
NT = (((1,), (1,)), ((), ()))
TN_DIMS = (((0,), (0,)), ((), ()))


def gelu_parts(pre):
    scale_c = 0.7978845608
    t = jnp.tanh(scale_c * (pre + 0.044715 * pre * pre * pre))
    value = 0.5 * pre * (1.0 + t)
    deriv = 0.5 * (1.0 + t) + 0.5 * pre * (1.0 - t * t) * scale_c * (
        1.0 + 3.0 * 0.044715 * pre * pre
    )
    return value, deriv


def weight_grads_kernel(tok, slo, hid, grd, o_in, o_out):
    o_in[...] = lax.dot_general(
        tok[...], slo[...], TN_DIMS, preferred_element_type=jnp.float32
    ).astype(jnp.bfloat16)
    o_out[...] = lax.dot_general(
        hid[...], grd[...], TN_DIMS, preferred_element_type=jnp.float32
    ).astype(jnp.bfloat16)


def weight_grads(tok, slo, hid, grd):
    rows, width = tok.shape
    units = slo.shape[1]
    steps = math.gcd(math.gcd(width // 128, units // 128), 12)
    tw, tu = width // steps, units // steps
    return pl.pallas_call(
        weight_grads_kernel,
        grid=(steps,),
        in_specs=[
            pl.BlockSpec((rows, tw), lambda i: (0, i)),
            pl.BlockSpec((rows, units), lambda i: (0, 0)),
            pl.BlockSpec((rows, tu), lambda i: (0, i)),
            pl.BlockSpec((rows, width), lambda i: (0, 0)),
        ],
        out_specs=[
            pl.BlockSpec((tw, units), lambda i: (i, 0)),
            pl.BlockSpec((tu, width), lambda i: (i, 0)),
        ],
        out_shape=[
            jax.ShapeDtypeStruct((width, units), jnp.bfloat16),
            jax.ShapeDtypeStruct((units, width), jnp.bfloat16),
        ],
        compiler_params=pltpu.CompilerParams(vmem_limit_bytes=48 * 1024 * 1024),
        cost_estimate=pl.CostEstimate(
            flops=4 * rows * width * units,
            bytes_accessed=4 * width * units,
            transcendentals=0,
        ),
    )(tok, slo, hid, grd)


def fused_kernel(
    sizes, tok_ref, grd_ref, win_hbm, wout_hbm,
    out_ref, gin_ref, tok_all, grd_all, hid_all, slo_all,
    win, wout, lhs, acc, part, rbuf, own, act, deriv,
    obuf, ohalf, yrecv, zf, zsend, zrecv,
    wsem, lsem, zss, zrs, yss, yrs, rss, rrs, ass, ars, css, crs, dss, drs,
):
    X, Y, Z = sizes["gx"], sizes["gy"], sizes["gz"]
    gx, gy, gz = lax.axis_index("gx"), lax.axis_index("gy"), lax.axis_index("gz")
    R, D = tok_ref.shape
    T, F = hid_all.shape
    C, H = T // X, Z * R
    TN = math.gcd(math.gcd(F, D), 768)
    NF, ND = F // TN, D // TN
    f32, bf16 = jnp.float32, jnp.bfloat16

    def to(axis, me, k):
        return {axis: lax.rem(me + k, sizes[axis])}

    def rem(src, dst, ss, rs, axis, me, k):
        return pltpu.make_async_remote_copy(
            src_ref=src, dst_ref=dst, send_sem=ss, recv_sem=rs,
            device_id=to(axis, me, k), device_id_type=MESH,
        )

    pltpu.make_async_copy(win_hbm, win, wsem.at[0]).start()
    pltpu.make_async_copy(wout_hbm, wout, wsem.at[1]).start()

    barrier = pltpu.get_barrier_semaphore()
    for axis, me in (("gx", gx), ("gy", gy), ("gz", gz)):
        for k in range(1, sizes[axis]):
            pl.semaphore_signal(barrier, inc=1, device_id=to(axis, me, k), device_id_type=MESH)
    pl.semaphore_wait(barrier, X + Y + Z - 3)

    srcs, alls = (tok_ref, grd_ref), (tok_all, grd_all)

    def block(ref, y, z):
        return ref.at[pl.ds(pl.multiple_of((y * Z + z) * R, 8), R)]

    def zcopy(a, k):
        return rem(srcs[a], block(alls[a], gy, gz), zss.at[a, k - 1], zrs.at[a, k - 1], "gz", gz, k)

    def zarrive(a, k):
        b = block(alls[a], gy, lax.rem(gz - k + Z, Z))
        return rem(b, b, zss.at[a, k - 1], zrs.at[a, k - 1], "gz", gz, k)

    def ycopy(a, p, j):
        b = block(alls[a], gy, lax.rem(gz - j + Z, Z))
        return rem(srcs[a] if j == 0 else b, b, yss.at[a, p - 1, j], yrs.at[a, p - 1, j], "gy", gy, p)

    def yarrive(a, p, j):
        b = block(alls[a], lax.rem(gy - p + Y, Y), lax.rem(gz - j + Z, Z))
        return rem(b, b, yss.at[a, p - 1, j], yrs.at[a, p - 1, j], "gy", gy, p)

    def mine(a):
        return pltpu.make_async_copy(srcs[a], block(alls[a], gy, gz), lsem.at[a])

    def gather_start(a):
        for k in range(Z - 1, 0, -1):
            zcopy(a, k).start()
        for p in range(1, Y):
            ycopy(a, p, 0).start()
        mine(a).start()

    def gather_forward(a):
        for j in range(1, Z):
            zarrive(a, j).wait_recv()
            for p in range(1, Y):
                ycopy(a, p, j).start()

    def gather_finish(a):
        mine(a).wait()
        for p in range(1, Y):
            for j in range(Z):
                yarrive(a, p, j).wait_recv()
        load = pltpu.make_async_copy(alls[a], lhs.at[a], lsem.at[2 + a])
        load.start()
        load.wait()

    def cols(t):
        return pl.ds(pl.multiple_of(t * TN, TN), TN)

    def chunk(i):
        return pl.ds(pl.multiple_of(i * C, 16), C)

    def half(i):
        return pl.ds(pl.multiple_of(i * H, 16), H)

    def rcopy(a, t, k):
        return rem(
            part.at[a, chunk(lax.rem(gx + k, X)), cols(t)], rbuf.at[a, k - 1, :, cols(t)],
            rss.at[a, t, k - 1], rrs.at[a, t, k - 1], "gx", gx, k,
        )

    def acopy(a, t, k):
        b = act.at[a, chunk(gx), cols(t)]
        return rem(b, b, ass.at[a, t, k - 1], ars.at[a, t, k - 1], "gx", gx, k)

    def aarrive(a, t, k):
        b = act.at[a, chunk(lax.rem(gx - k + X, X)), cols(t)]
        return rem(b, b, ass.at[a, t, k - 1], ars.at[a, t, k - 1], "gx", gx, k)

    def ccopy(a, n, p):
        return rem(
            obuf.at[a, half(lax.rem(gy + p, Y)), cols(n)], yrecv.at[a, p - 1, :, cols(n)],
            css.at[a, n, p - 1], crs.at[a, n, p - 1], "gy", gy, p,
        )

    def dcopy(a, n, k):
        return rem(
            zsend.at[a, lax.rem(gz + k, Z), :, cols(n)], zrecv.at[a, k - 1, :, cols(n)],
            dss.at[a, n, k - 1], drs.at[a, n, k - 1], "gz", gz, k,
        )

    def loop(n, body):
        lax.fori_loop(0, n, lambda i, c: (body(i), c)[1], 0)

    def up(a, w, transposed):
        def body(t):
            if transposed:
                acc[...] = lax.dot_general(lhs[a], w[cols(t), :], NT, preferred_element_type=f32)
            else:
                acc[...] = lax.dot_general(lhs[a], w[:, cols(t)], NN, preferred_element_type=f32)
            part[a, :, cols(t)] = acc[...].astype(bf16)
            own[a, :, cols(t)] = acc[chunk(gx), :]
            for k in range(1, X):
                rcopy(a, t, k).start()
        loop(NF, body)

    def summed(a, t):
        for k in range(1, X):
            rcopy(a, t, k).wait_recv()
        total = own[a, :, cols(t)]
        for k in range(1, X):
            total = total + rbuf[a, k - 1, :, cols(t)].astype(f32)
        return total

    def publish(a, t, value):
        act[a, chunk(gx), cols(t)] = value.astype(bf16)
        for k in range(1, X):
            acopy(a, t, k).start()

    gather_start(0)
    gather_forward(0)
    gather_start(1)
    gather_finish(0)
    pltpu.make_async_copy(win_hbm, win, wsem.at[0]).wait()
    up(0, win, False)
    gather_forward(1)
    gather_finish(1)
    pltpu.make_async_copy(wout_hbm, wout, wsem.at[1]).wait()
    up(1, wout, True)

    def hidden_step(t):
        value, slope = gelu_parts(summed(0, t))
        deriv[:, cols(t)] = slope
        publish(0, t, value)

    loop(NF, hidden_step)
    loop(NF, lambda t: publish(1, t, summed(1, t) * deriv[:, cols(t)]))

    keeps = (hid_all, slo_all)

    def scatter_step(a, n):
        for p in range(1, Y):
            ccopy(a, n, p).wait_recv()
        total = ohalf[a, :, cols(n)]
        for p in range(1, Y):
            total = total + yrecv[a, p - 1, :, cols(n)].astype(f32)
        for z in range(Z):
            rows = total[z * R : (z + 1) * R]
            zf[a, z, :, cols(n)] = rows
            zsend[a, z, :, cols(n)] = rows.astype(bf16)
        for k in range(1, Z):
            dcopy(a, n, k).start()

    def down(a, w, transposed):
        def arrive(t):
            for k in range(1, X):
                aarrive(a, t, k).wait_recv()
        loop(NF, arrive)
        pltpu.make_async_copy(act.at[a], keeps[a], lsem.at[4 + a]).start()

        def body(n):
            if transposed:
                acc[...] = lax.dot_general(act[a], w[cols(n), :], NT, preferred_element_type=f32)
            else:
                acc[...] = lax.dot_general(act[a], w[:, cols(n)], NN, preferred_element_type=f32)
            obuf[a, :, cols(n)] = acc[...].astype(bf16)
            ohalf[a, :, cols(n)] = acc[half(gy), :]
            for p in range(1, Y):
                ccopy(a, n, p).start()

            @pl.when(n >= 1)
            def _():
                scatter_step(a, n - 1)
        loop(ND, body)
        scatter_step(a, ND - 1)

    down(0, wout, False)
    down(1, win, True)

    for a, ref in ((0, out_ref), (1, gin_ref)):
        def last(n, a=a, ref=ref):
            for k in range(1, Z):
                dcopy(a, n, k).wait_recv()
            total = zf[a, gz, :, cols(n)]
            for k in range(1, Z):
                total = total + zrecv[a, k - 1, :, cols(n)].astype(f32)
            ref[:, cols(n)] = total
        loop(ND, last)

    for a in range(2):
        pltpu.make_async_copy(act.at[a], keeps[a], lsem.at[4 + a]).wait()
        for k in range(1, Z):
            zcopy(a, k).wait_send()
        for p in range(1, Y):
            for j in range(Z):
                ycopy(a, p, j).wait_send()

        def drain_f(t, a=a):
            for k in range(1, X):
                rcopy(a, t, k).wait_send()
                acopy(a, t, k).wait_send()
        loop(NF, drain_f)

        def drain_d(n, a=a):
            for p in range(1, Y):
                ccopy(a, n, p).wait_send()
            for k in range(1, Z):
                dcopy(a, n, k).wait_send()
        loop(ND, drain_d)


def shards(sizes, tokens, grad_out, w_in, w_out):
    X, Y, Z = sizes["gx"], sizes["gy"], sizes["gz"]
    R, D = tokens.shape
    F = w_in.shape[1]
    T = R * Y * Z
    C, H = T // X, Z * R
    TN = math.gcd(math.gcd(F, D), 768)
    NF, ND = F // TN, D // TN
    f32, bf16 = jnp.float32, jnp.bfloat16
    dma = pltpu.SemaphoreType.DMA
    any_spec = pl.BlockSpec(memory_space=pl.ANY)
    vmem_spec = pl.BlockSpec(memory_space=pltpu.VMEM)
    out, gin, tok, grd, hid, slo = pl.pallas_call(
        functools.partial(fused_kernel, sizes),
        in_specs=[any_spec] * 4,
        out_specs=[vmem_spec] * 2 + [any_spec] * 4,
        out_shape=[
            jax.ShapeDtypeStruct((R, D), f32),
            jax.ShapeDtypeStruct((R, D), f32),
            jax.ShapeDtypeStruct((T, D), bf16),
            jax.ShapeDtypeStruct((T, D), bf16),
            jax.ShapeDtypeStruct((T, F), bf16),
            jax.ShapeDtypeStruct((T, F), bf16),
        ],
        scratch_shapes=[
            pltpu.VMEM((D, F), bf16),
            pltpu.VMEM((F, D), bf16),
            pltpu.VMEM((2, T, D), bf16),
            pltpu.VMEM((T, TN), f32),
            pltpu.VMEM((2, T, F), bf16),
            pltpu.VMEM((2, X - 1, C, F), bf16),
            pltpu.VMEM((2, C, F), f32),
            pltpu.VMEM((2, T, F), bf16),
            pltpu.VMEM((C, F), f32),
            pltpu.VMEM((2, T, D), bf16),
            pltpu.VMEM((2, H, D), f32),
            pltpu.VMEM((2, Y - 1, H, D), bf16),
            pltpu.VMEM((2, Z, R, D), f32),
            pltpu.VMEM((2, Z, R, D), bf16),
            pltpu.VMEM((2, Z - 1, R, D), bf16),
            dma((2,)),
            dma((6,)),
            dma((2, Z - 1)),
            dma((2, Z - 1)),
            dma((2, Y - 1, Z)),
            dma((2, Y - 1, Z)),
            dma((2, NF, X - 1)),
            dma((2, NF, X - 1)),
            dma((2, NF, X - 1)),
            dma((2, NF, X - 1)),
            dma((2, ND, Y - 1)),
            dma((2, ND, Y - 1)),
            dma((2, ND, Z - 1)),
            dma((2, ND, Z - 1)),
        ],
        compiler_params=pltpu.CompilerParams(
            collective_id=0, has_side_effects=True,
            vmem_limit_bytes=63 * 1024 * 1024,
        ),
    )(tokens, grad_out, w_in, w_out)
    g_in, g_out = weight_grads(tok, slo, hid, grd)
    return out, gin, g_in, g_out


def solution(mesh):
    rows = P(("gy", "gz"), "gx")
    w_in = P("gx", ("gy", "gz"))
    return jax.shard_map(
        functools.partial(shards, dict(mesh.shape)),
        mesh=mesh,
        in_specs=(rows, rows, w_in, rows),
        out_specs=(rows, rows, w_in, rows),
        check_vma=False,
    )
```

time: 316 us -> 118 us (0.37)
  waiting for transfers between devices: 201 us -> 0 us
  Pallas kernels: 0 us -> 110 us
  matrix products: 71.1 us -> 0 us
  local copies, waits for them, and re-layouts: 26.1 us -> 6.51 us
  between operations: 13.8 us -> 0.65 us
    psum x1 -> x0, waiting for transfers between devices: 113 us -> none  [shards(): pre_sum, back_sum = lax.psum((pre_part, back_part), 'gx')]
    pallas_call x0 -> x2, Pallas kernels: none -> 110 us  [the longest x1 95.7 us: shards(): pl.pallas_call(functools.partial(fused_kernel, sizes), in_specs=[any_spec...]
    dot_general x6 -> x0, matrix products: 71.1 us -> none  [the longest x2 26.2 us: right_product(): lax.dot_general(left, right, (((1,), (1,)), ((), ())), preferred_element_...]
    reduce_scatter x2 -> x0, waiting for transfers between devices: 48.5 us -> none  [the longest x1 48.5 us: shards(): lax.psum_scatter(right_product(picked, w_in), ('gy', 'gz'), scatter_dimen...]
    all_gather x2 -> x0, waiting for transfers between devices: 38.4 us -> none  [the longest x1 26.3 us: shards(): lax.all_gather(tokens, ('gy', 'gz'), axis=0, tiled=True)]
    unnamed x5 -> x14, local copies, waits for them, and re-layouts: 26.1 us -> 6.51 us
  transfers between devices with their start and end apart: 5 -> 0, of which waited for: 4 -> 0; matrix products, arithmetic and copies ran while one was open for 23% -> 0% of each run, Pallas kernels for 0% -> 0%
where the time goes in v1:
time: 118 us; the launch traced here: 117 us
  Pallas kernels  110 us (93%)
  local copies, waits for them, and re-layouts  6.51 us (6%)
    pallas_call x1, Pallas kernels, shards(): pl.pallas_call(functools.partial(fused_kernel, sizes), in_specs=[any_spec...  95.7 us
    pallas_call x1, Pallas kernels, weight_grads(): pl.pallas_call(weight_grads_kernel, grid=(steps,), in_specs=[pl.BlockSpec...  14.5 us
    unnamed x14, local copies, waits for them, and re-layouts  6.51 us

profile of v1, /device:TPU:0, one launch (start us, length us, event | category | flops | bytes accessed | tf_op | source)
XLA Modules:
  0.0 117.4 jit_solution(14257804789233145607)
XLA Ops:
  0.6 95.7 %shard_map.75 = (f32[24,3072]{1,0:T(8,128)}, f32[24,3072]{1,0:T(8,128)}, bf16[192,3072]{1,0:T(8,128)(2,1)}, bf16[192,3072]{1,0:T(8,128)(2,1)}, bf16[192,3072]{1,0:T(8,128)(2,1)}, /*index=5*/bf16[192,3072]{1,0:T(8,128)(2,1)}) custom-call(bf16[24,3072]{1,0:T(8,128)(2,1)} %tok_ref.1, bf16[24,3072]{1,0:T(8,128)(2,1)} %grd_ref.1, bf16[3072,3072]{1,0:T(8,128)(2,1)} %win_hbm.1, ...), custom_call_target="tpu_custom_call" | custom-call | tf_op jit(solution)/shard_map/pallas_call | solution.py:313
  96.3 0.0 copy-start
  96.3 1.3 %copy-done = bf16[192,3072]{1,0:T(8,128)(2,1)S(1)} copy-done((bf16[192,3072]{1,0:T(8,128)(2,1)S(1)}, bf16[192,3072]{1,0:T(8,128)(2,1)}, u32[]{:S(2)}) %copy-start) | copy-done | bytes 1179672
  97.6 0.0 copy-start.1
  97.6 1.3 %copy-done.1 = bf16[192,3072]{1,0:T(8,128)(2,1)S(1)} copy-done((bf16[192,3072]{1,0:T(8,128)(2,1)S(1)}, bf16[192,3072]{1,0:T(8,128)(2,1)}, u32[]{:S(2)}) %copy-start.1) | copy-done | bytes 1179672
  98.9 0.0 copy-start.2
  98.9 1.3 %copy-done.2 = bf16[192,3072]{1,0:T(8,128)(2,1)S(1)} copy-done((bf16[192,3072]{1,0:T(8,128)(2,1)S(1)}, bf16[192,3072]{1,0:T(8,128)(2,1)}, u32[]{:S(2)}) %copy-start.2) | copy-done | bytes 1179672
  100.1 0.0 copy-start.3
  100.2 1.3 %copy-done.3 = bf16[192,3072]{1,0:T(8,128)(2,1)S(1)} copy-done((bf16[192,3072]{1,0:T(8,128)(2,1)S(1)}, bf16[192,3072]{1,0:T(8,128)(2,1)}, u32[]{:S(2)}) %copy-start.3) | copy-done | bytes 1179672
  101.4 0.0 copy-start.5
  101.4 0.0 copy-start.4
  101.4 14.5 %shard_map.76 = (bf16[3072,3072]{1,0:T(8,128)(2,1)}, bf16[3072,3072]{1,0:T(8,128)(2,1)}) custom-call(bf16[192,3072]{1,0:T(8,128)(2,1)S(1)} %copy-done, bf16[192,3072]{1,0:T(8,128)(2,1)S(1)} %copy-done.3, bf16[192,3072]{1,0:T(8,128)(2,1)S(1)} %copy-done.2, bf16[192,3072]{1,0:T(8,128)(2,1)S(1)} %copy-done.1), custom_call_target="tpu_custom_call" | custom-call | flops 7247757312 | bytes 37748736 | tf_op jit(solution)/shard_map/pallas_call | solution.py:41
  116.0 0.0 copy-done.5
  116.0 0.7 copy.10
  116.7 0.0 copy-done.4
  116.7 0.7 copy.11
Async XLA Ops:
  96.3 1.3 %copy-start = (bf16[192,3072]{1,0:T(8,128)(2,1)S(1)}, bf16[192,3072]{1,0:T(8,128)(2,1)}, u32[]{:S(2)}) copy-start(bf16[192,3072]{1,0:T(8,128)(2,1)} %get-tuple-element.14.tok) | copy-start | bytes 3538948
  97.6 1.3 %copy-start.1 = (bf16[192,3072]{1,0:T(8,128)(2,1)S(1)}, bf16[192,3072]{1,0:T(8,128)(2,1)}, u32[]{:S(2)}) copy-start(bf16[192,3072]{1,0:T(8,128)(2,1)} %get-tuple-element.17.grd) | copy-start | bytes 3538948
  98.9 1.3 %copy-start.2 = (bf16[192,3072]{1,0:T(8,128)(2,1)S(1)}, bf16[192,3072]{1,0:T(8,128)(2,1)}, u32[]{:S(2)}) copy-start(bf16[192,3072]{1,0:T(8,128)(2,1)} %get-tuple-element.16.hid) | copy-start | bytes 3538948
  100.1 1.3 %copy-start.3 = (bf16[192,3072]{1,0:T(8,128)(2,1)S(1)}, bf16[192,3072]{1,0:T(8,128)(2,1)}, u32[]{:S(2)}) copy-start(bf16[192,3072]{1,0:T(8,128)(2,1)} %get-tuple-element.15.slo) | copy-start | bytes 3538948
  101.4 14.5 %copy-start.5 = (f32[24,3072]{1,0:T(8,128)S(1)}, f32[24,3072]{1,0:T(8,128)}, u32[]{:S(2)}) copy-start(f32[24,3072]{1,0:T(8,128)} %get-tuple-element.24) | copy-start | bytes 884740
  101.4 15.3 %copy-start.4 = (f32[24,3072]{1,0:T(8,128)S(1)}, f32[24,3072]{1,0:T(8,128)}, u32[]{:S(2)}) copy-start(f32[24,3072]{1,0:T(8,128)} %get-tuple-element.25) | copy-start | bytes 884740

commit v2 on v1

--- a/solution.py
+++ b/solution.py
@@ -55,7 +55,7 @@
             jax.ShapeDtypeStruct((width, units), jnp.bfloat16),
             jax.ShapeDtypeStruct((units, width), jnp.bfloat16),
         ],
-        compiler_params=pltpu.CompilerParams(vmem_limit_bytes=48 * 1024 * 1024),
+        compiler_params=pltpu.CompilerParams(vmem_limit_bytes=62 * 1024 * 1024),
         cost_estimate=pl.CostEstimate(
             flops=4 * rows * width * units,
             bytes_accessed=4 * width * units,
@@ -64,13 +64,13 @@
     )(tok, slo, hid, grd)
 
 
-def fused_kernel(
-    sizes, tok_ref, grd_ref, win_hbm, wout_hbm,
-    out_ref, gin_ref, tok_all, grd_all, hid_all, slo_all,
-    win, wout, lhs, acc, part, rbuf, own, act, deriv,
+def fused_kernel(sizes, tok_ref, grd_ref, win_hbm, wout_hbm, *refs):
+    gsends, refs = refs[: sizes["gz"] - 1], refs[sizes["gz"] - 1 :]
+    (out_ref, gown_ref, tok_all, grd_all, hid_all, slo_all,
+    win, wout, lhs, acc, part, dbuf, rbuf, own, act, deriv,
     obuf, ohalf, yrecv, zf, zsend, zrecv,
-    wsem, lsem, zss, zrs, yss, yrs, rss, rrs, ass, ars, css, crs, dss, drs,
-):
+    wsem, lsem, zss, zrs, yss, yrs, rss, rrs, ass, ars, css, crs, dss, drs) = refs
+
     X, Y, Z = sizes["gx"], sizes["gy"], sizes["gz"]
     gx, gy, gz = lax.axis_index("gx"), lax.axis_index("gy"), lax.axis_index("gz")
     R, D = tok_ref.shape
@@ -152,19 +152,68 @@
     def half(i):
         return pl.ds(pl.multiple_of(i * H, 16), H)
 
-    def rcopy(a, t, k):
-        return rem(
-            part.at[a, chunk(lax.rem(gx + k, X)), cols(t)], rbuf.at[a, k - 1, :, cols(t)],
-            rss.at[a, t, k - 1], rrs.at[a, t, k - 1], "gx", gx, k,
+    def left(t):
+        return pl.ds(pl.multiple_of(t * TN, TN // 2), TN // 2)
+
+    def right(t):
+        return pl.ds(pl.multiple_of(t * TN + TN // 2, TN // 2), TN // 2)
+
+    def hop(src, dst, sems, a, t, i, mask):
+        return pltpu.make_async_remote_copy(
+            src_ref=src, dst_ref=dst, send_sem=sems[0].at[a, t, i], recv_sem=sems[1].at[a, t, i],
+            device_id={"gx": peer(mask)}, device_id_type=MESH,
         )
 
-    def acopy(a, t, k):
+    def peer(mask):
+        low = lax.rem(gx, 2)
+        high = gx - low
+        if mask & 1:
+            low = 1 - low
+        if mask & 2:
+            high = 2 - high
+        return high + low
+
+    def diagonal(a, t, i):
+        c = (left, right)[i](t)
+        return hop(part.at[a, chunk(peer(3)), c], dbuf.at[a, :, c], (rss, rrs), a, t, i, i + 1)
+
+    def direct(a, t, i):
+        c = (left, right)[i](t)
+        return hop(part.at[a, chunk(peer(i + 1)), c], rbuf.at[a, i, :, c], (rss, rrs), a, t, 2 + i, i + 1)
+
+    def relay(a, t, i):
+        c = (right, left)[i](t)
+        return hop(part.at[a, chunk(peer(i + 1)), c], rbuf.at[a, i, :, c], (rss, rrs), a, t, 4 + i, i + 1)
+
+    def relay_step(a, t):
+        for i in range(2):
+            diagonal(a, t, i).wait_recv()
+            c = (left, right)[i](t)
+            rows = chunk(peer(2 - i))
+            term = part[a, rows, c].astype(f32) + dbuf[a, :, c].astype(f32)
+            part[a, rows, c] = term.astype(bf16)
+            relay(a, t, 1 - i).start()
+
+    def acopy(a, t, i):
         b = act.at[a, chunk(gx), cols(t)]
-        return rem(b, b, ass.at[a, t, k - 1], ars.at[a, t, k - 1], "gx", gx, k)
-
-    def aarrive(a, t, k):
-        b = act.at[a, chunk(lax.rem(gx - k + X, X)), cols(t)]
-        return rem(b, b, ass.at[a, t, k - 1], ars.at[a, t, k - 1], "gx", gx, k)
+        return hop(b, b, (ass, ars), a, t, i, i + 1)
+
+    def aarrive(a, t, i):
+        b = act.at[a, chunk(peer(i + 1)), cols(t)]
+        return hop(b, b, (ass, ars), a, t, i, i + 1)
+
+    def apass(a, t, i):
+        b = act.at[a, chunk(peer(2 - i)), (right, left)[i](t)]
+        return hop(b, b, (ass, ars), a, t, 2 + i, i + 1)
+
+    def apassed(a, t, i):
+        b = act.at[a, chunk(peer(3)), (right, left)[i](t)]
+        return hop(b, b, (ass, ars), a, t, 2 + i, i + 1)
+
+    def pass_step(a, t):
+        for i in range(2):
+            aarrive(a, t, i).wait_recv()
+            apass(a, t, 1 - i).start()
 
     def ccopy(a, n, p):
         return rem(
@@ -172,10 +221,10 @@
             css.at[a, n, p - 1], crs.at[a, n, p - 1], "gy", gy, p,
         )
 
-    def dcopy(a, n, k):
+    def dcopy(n, k):
         return rem(
-            zsend.at[a, lax.rem(gz + k, Z), :, cols(n)], zrecv.at[a, k - 1, :, cols(n)],
-            dss.at[a, n, k - 1], drs.at[a, n, k - 1], "gz", gz, k,
+            zsend.at[lax.rem(gz + k, Z), :, cols(n)], zrecv.at[k - 1, :, cols(n)],
+            dss.at[n, k - 1], drs.at[n, k - 1], "gz", gz, k,
         )
 
     def loop(n, body):
@@ -189,22 +238,30 @@
                 acc[...] = lax.dot_general(lhs[a], w[:, cols(t)], NN, preferred_element_type=f32)
             part[a, :, cols(t)] = acc[...].astype(bf16)
             own[a, :, cols(t)] = acc[chunk(gx), :]
-            for k in range(1, X):
-                rcopy(a, t, k).start()
+            for i in range(2):
+                diagonal(a, t, i).start()
+            for i in range(2):
+                direct(a, t, i).start()
+
+            @pl.when(t >= 1)
+            def _():
+                relay_step(a, t - 1)
         loop(NF, body)
+        relay_step(a, NF - 1)
 
     def summed(a, t):
-        for k in range(1, X):
-            rcopy(a, t, k).wait_recv()
+        for i in range(2):
+            direct(a, t, i).wait_recv()
+            relay(a, t, i).wait_recv()
         total = own[a, :, cols(t)]
-        for k in range(1, X):
-            total = total + rbuf[a, k - 1, :, cols(t)].astype(f32)
+        for i in range(2):
+            total = total + rbuf[a, i, :, cols(t)].astype(f32)
         return total
 
     def publish(a, t, value):
         act[a, chunk(gx), cols(t)] = value.astype(bf16)
-        for k in range(1, X):
-            acopy(a, t, k).start()
+        for i in range(2):
+            acopy(a, t, i).start()
 
     gather_start(0)
     gather_forward(0)
@@ -223,7 +280,12 @@
         publish(0, t, value)
 
     loop(NF, hidden_step)
-    loop(NF, lambda t: publish(1, t, summed(1, t) * deriv[:, cols(t)]))
+
+    def slopes_step(t):
+        publish(1, t, summed(1, t) * deriv[:, cols(t)])
+        pass_step(0, t)
+
+    loop(NF, slopes_step)
 
     keeps = (hid_all, slo_all)
 
@@ -236,14 +298,20 @@
         for z in range(Z):
             rows = total[z * R : (z + 1) * R]
             zf[a, z, :, cols(n)] = rows
-            zsend[a, z, :, cols(n)] = rows.astype(bf16)
+            if a == 0:
+                zsend[z, :, cols(n)] = rows.astype(bf16)
         for k in range(1, Z):
-            dcopy(a, n, k).start()
+            if a == 0:
+                dcopy(n, k).start()
+            else:
+                gsends[k - 1][:, cols(n)] = zf[a, lax.rem(gz + k, Z), :, cols(n)].astype(bf16)
+        if a == 1:
+            gown_ref[:, cols(n)] = zf[a, gz, :, cols(n)]
 
     def down(a, w, transposed):
         def arrive(t):
-            for k in range(1, X):
-                aarrive(a, t, k).wait_recv()
+            for i in range(2):
+                apassed(a, t, i).wait_recv()
         loop(NF, arrive)
         pltpu.make_async_copy(act.at[a], keeps[a], lsem.at[4 + a]).start()
 
@@ -260,21 +328,27 @@
             @pl.when(n >= 1)
             def _():
                 scatter_step(a, n - 1)
+            if a == 0:
+                @pl.when(n < NF)
+                def _():
+                    pass_step(1, n)
         loop(ND, body)
+        if a == 0:
+            for t in range(ND, NF):
+                pass_step(1, t)
         scatter_step(a, ND - 1)
 
     down(0, wout, False)
     down(1, win, True)
 
-    for a, ref in ((0, out_ref), (1, gin_ref)):
-        def last(n, a=a, ref=ref):
-            for k in range(1, Z):
-                dcopy(a, n, k).wait_recv()
-            total = zf[a, gz, :, cols(n)]
-            for k in range(1, Z):
-                total = total + zrecv[a, k - 1, :, cols(n)].astype(f32)
-            ref[:, cols(n)] = total
-        loop(ND, last)
+    def last(n):
+        for k in range(1, Z):
+            dcopy(n, k).wait_recv()
+        total = zf[0, gz, :, cols(n)]
+        for k in range(1, Z):
+            total = total + zrecv[k - 1, :, cols(n)].astype(f32)
+        out_ref[:, cols(n)] = total
+    loop(ND, last)
 
     for a in range(2):
         pltpu.make_async_copy(act.at[a], keeps[a], lsem.at[4 + a]).wait()
@@ -285,16 +359,20 @@
                 ycopy(a, p, j).wait_send()
 
         def drain_f(t, a=a):
-            for k in range(1, X):
-                rcopy(a, t, k).wait_send()
-                acopy(a, t, k).wait_send()
+            for i in range(2):
+                diagonal(a, t, i).wait_send()
+                direct(a, t, i).wait_send()
+                relay(a, t, i).wait_send()
+                acopy(a, t, i).wait_send()
+                apass(a, t, i).wait_send()
         loop(NF, drain_f)
 
         def drain_d(n, a=a):
             for p in range(1, Y):
                 ccopy(a, n, p).wait_send()
-            for k in range(1, Z):
-                dcopy(a, n, k).wait_send()
+            if a == 0:
+                for k in range(1, Z):
+                    dcopy(n, k).wait_send()
         loop(ND, drain_d)
 
 
@@ -310,11 +388,12 @@
     dma = pltpu.SemaphoreType.DMA
     any_spec = pl.BlockSpec(memory_space=pl.ANY)
     vmem_spec = pl.BlockSpec(memory_space=pltpu.VMEM)
-    out, gin, tok, grd, hid, slo = pl.pallas_call(
+    assert X == 4
+    *sends, out, gin, tok, grd, hid, slo = pl.pallas_call(
         functools.partial(fused_kernel, sizes),
         in_specs=[any_spec] * 4,
-        out_specs=[vmem_spec] * 2 + [any_spec] * 4,
-        out_shape=[
+        out_specs=[vmem_spec] * (Z + 1) + [any_spec] * 4,
+        out_shape=[jax.ShapeDtypeStruct((R, D), bf16)] * (Z - 1) + [
             jax.ShapeDtypeStruct((R, D), f32),
             jax.ShapeDtypeStruct((R, D), f32),
             jax.ShapeDtypeStruct((T, D), bf16),
@@ -328,7 +407,8 @@
             pltpu.VMEM((2, T, D), bf16),
             pltpu.VMEM((T, TN), f32),
             pltpu.VMEM((2, T, F), bf16),
-            pltpu.VMEM((2, X - 1, C, F), bf16),
+            pltpu.VMEM((2, C, F), bf16),
+            pltpu.VMEM((2, 2, C, F), bf16),
             pltpu.VMEM((2, C, F), f32),
             pltpu.VMEM((2, T, F), bf16),
             pltpu.VMEM((C, F), f32),
@@ -336,29 +416,35 @@
             pltpu.VMEM((2, H, D), f32),
             pltpu.VMEM((2, Y - 1, H, D), bf16),
             pltpu.VMEM((2, Z, R, D), f32),
-            pltpu.VMEM((2, Z, R, D), bf16),
-            pltpu.VMEM((2, Z - 1, R, D), bf16),
+            pltpu.VMEM((Z, R, D), bf16),
+            pltpu.VMEM((Z - 1, R, D), bf16),
             dma((2,)),
             dma((6,)),
             dma((2, Z - 1)),
             dma((2, Z - 1)),
             dma((2, Y - 1, Z)),
             dma((2, Y - 1, Z)),
-            dma((2, NF, X - 1)),
-            dma((2, NF, X - 1)),
-            dma((2, NF, X - 1)),
-            dma((2, NF, X - 1)),
+            dma((2, NF, 6)),
+            dma((2, NF, 6)),
+            dma((2, NF, 4)),
+            dma((2, NF, 4)),
             dma((2, ND, Y - 1)),
             dma((2, ND, Y - 1)),
-            dma((2, ND, Z - 1)),
-            dma((2, ND, Z - 1)),
+            dma((ND, Z - 1)),
+            dma((ND, Z - 1)),
         ],
         compiler_params=pltpu.CompilerParams(
             collective_id=0, has_side_effects=True,
             vmem_limit_bytes=63 * 1024 * 1024,
         ),
     )(tokens, grad_out, w_in, w_out)
+    moved = [
+        lax.ppermute(sends[k - 1], "gz", [(z, (z + k) % Z) for z in range(Z)])
+        for k in range(1, Z)
+    ]
     g_in, g_out = weight_grads(tok, slo, hid, grd)
+    for m in moved:
+        gin = gin + m.astype(f32)
     return out, gin, g_in, g_out
 
 

time: 118 us -> 109 us (0.924)
  Pallas kernels: 110 us -> 102 us
  local copies, waits for them, and re-layouts: 6.51 us -> 0.72 us
  starting transfers between devices: 0 us -> 4.17 us
    pallas_call x1, Pallas kernels: 95.7 us -> 85.6 us  [shards(): pl.pallas_call(functools.partial(fused_kernel, sizes), in_specs=[any_spec...]
    unnamed x14 -> x5, local copies, waits for them, and re-layouts: 6.51 us -> 0.72 us
    ppermute x0 -> x3, starting transfers between devices: none -> 4.17 us  [shards(): lax.ppermute(sends[k - 1], 'gz', [(z, (z + k) % Z) for z in range(Z)])]
    pallas_call x1, Pallas kernels: 14.5 us -> 16.4 us  [weight_grads(): pl.pallas_call(weight_grads_kernel, grid=(steps,), in_specs=[pl.BlockSpec...]
  transfers between devices with their start and end apart: 0 -> 3, of which waited for: 0 -> 0; matrix products, arithmetic and copies ran while one was open for 0% -> 0% of each run, Pallas kernels for 0% -> 15%
where the time goes in v2:
time: 109 us; the launch traced here: 108 us
  Pallas kernels  102 us (94%)
  starting transfers between devices  4.17 us (4%)
    pallas_call x1, Pallas kernels, shards(): pl.pallas_call(functools.partial(fused_kernel, sizes), in_specs=[any_spec...  85.6 us
    pallas_call x1, Pallas kernels, weight_grads(): pl.pallas_call(weight_grads_kernel, grid=(steps,), in_specs=[pl.BlockSpec...  16.4 us
    ppermute x3, starting transfers between devices, shards(): lax.ppermute(sends[k - 1], 'gz', [(z, (z + k) % Z) for z in range(Z)])  4.17 us
  transfers between devices with their start and end apart: 3, of which 0 were waited for; matrix products, arithmetic and copies ran while one was open for 0% of the time, Pallas kernels for 15%

profile of v2, /device:TPU:0, one launch (start us, length us, event | category | flops | bytes accessed | tf_op | source)
XLA Modules:
  0.0 108.3 jit_solution(4256268905033508610)
XLA Ops:
  0.6 85.6 %shard_map.75 = (bf16[24,3072]{1,0:T(8,128)(2,1)}, bf16[24,3072]{1,0:T(8,128)(2,1)}, bf16[24,3072]{1,0:T(8,128)(2,1)}, f32[24,3072]{1,0:T(8,128)}, f32[24,3072]{...) custom-call(bf16[24,3072]{1,0:T(8,128)(2,1)} %tok_ref.1, ...), custom_call_target="tpu_custom_call" | custom-call | tf_op jit(solution)/shard_map/pallas_call | solution.py:392
  86.3 0.0 copy-start.1
  86.3 0.0 copy-start
  86.3 0.6 collective-permute-start
  86.9 0.9 collective-permute-start.1
  87.8 2.6 %collective-permute-start.2 = (bf16[24,3072]{1,0:T(8,128)(2,1)}, bf16[24,3072]{1,0:T(8,128)(2,1)S(1)}, u32[]{:S(2)}, u32[]{:S(2)}) collective-permute-start(bf16[24,3072]{1,0:T(8,128)(2,1)} %get-tuple-element.19), channel_id=1, source_target_pairs={{0,3},{1,0},{2,1},{3,2},{4,7},{5,4},{6,5},{7,6},{8,11},{9,8},{10,9... | collective-permute-start | bytes 442376 | tf_op jit(solution)/shard_map/ppermute | solution.py:442
  90.5 16.4 %shard_map.76 = (bf16[3072,3072]{1,0:T(8,128)(2,1)}, bf16[3072,3072]{1,0:T(8,128)(2,1)}) custom-call(bf16[192,3072]{1,0:T(8,128)(2,1)} %get-tuple-element.20.tok, bf16[192,3072]{1,0:T(8,128)(2,1)} %get-tuple-element.21.slo, bf16[192,3072]{1,0:T(8,128)(2,1)} %get-tuple-element.22.hid, bf16[192,3072]{1,0:T(8,128)(2,1)} %get-tuple-element.23.grd), custom_call_target="tpu_custom_call" | custom-call | flops 7247757312 | bytes 37748736 | tf_op jit(solution)/shard_map/pallas_call | solution.py:41
  106.8 0.0 collective-permute-done
  106.8 0.0 collective-permute-done.1
  106.8 0.0 collective-permute-done.2
  106.8 0.0 copy-done.1
  106.8 0.8 convert_add_fusion
  107.6 0.0 copy-done
  107.6 0.7 copy.9
Async XLA Ops:
  86.3 20.6 %copy-start.1 = (f32[24,3072]{1,0:T(8,128)S(1)}, f32[24,3072]{1,0:T(8,128)}, u32[]{:S(2)}) copy-start(f32[24,3072]{1,0:T(8,128)} %get-tuple-element.16) | copy-start | bytes 884740
  86.3 21.4 %copy-start = (f32[24,3072]{1,0:T(8,128)S(1)}, f32[24,3072]{1,0:T(8,128)}, u32[]{:S(2)}) copy-start(f32[24,3072]{1,0:T(8,128)} %get-tuple-element.30) | copy-start | bytes 884740
  86.3 20.5 %collective-permute-start = (bf16[24,3072]{1,0:T(8,128)(2,1)}, bf16[24,3072]{1,0:T(8,128)(2,1)S(1)}, u32[]{:S(2)}, u32[]{:S(2)}) collective-permute-start(bf16[24,3072]{1,0:T(8,128)(2,1)} %get-tuple-element.17), channel_id=1, source_target_pairs={{0,1},{1,2},{2,3},{3,0},{4,5},{5,6},{6,7},{7,4},{8,9},{9,10},{10,1... | collective-permute-start | bytes 442376 | tf_op jit(solution)/shard_map/ppermute | solution.py:442
  86.9 19.9 %collective-permute-start.1 = (bf16[24,3072]{1,0:T(8,128)(2,1)}, bf16[24,3072]{1,0:T(8,128)(2,1)S(1)}, u32[]{:S(2)}, u32[]{:S(2)}) collective-permute-start(bf16[24,3072]{1,0:T(8,128)(2,1)} %get-tuple-element.18), channel_id=1, source_target_pairs={{0,2},{1,3},{2,0},{3,1},{4,6},{5,7},{6,4},{7,5},{8,10},{9,11},{10,... | collective-permute-start | bytes 442376 | tf_op jit(solution)/shard_map/ppermute | solution.py:442
  87.8 19.0 %collective-permute-start.2 = (bf16[24,3072]{1,0:T(8,128)(2,1)}, bf16[24,3072]{1,0:T(8,128)(2,1)S(1)}, u32[]{:S(2)}, u32[]{:S(2)}) collective-permute-start(bf16[24,3072]{1,0:T(8,128)(2,1)} %get-tuple-element.19), channel_id=1, source_target_pairs={{0,3},{1,0},{2,1},{3,2},{4,7},{5,4},{6,5},{7,6},{8,11},{9,8},{10,9... | collective-permute-start | bytes 442376 | tf_op jit(solution)/shard_map/ppermute | solution.py:442
